TPU v7x, 128 devices: a whole 4x4x4 slice. The times are simulated.
128 devices in a mesh: cell: 32 (over x, z, y_hi), spec: 4 (over y_lo, core).
Axes of the slice: x: 4, y: 4 (y_hi: 2, y_lo: 2; y = y_hi * 2 + y_lo), z: 4, core: 2. Of those that a mesh axis runs over, the one named last changes fastest.
Arguments:
- fields: bfloat16 [4, 1024, 384], P('spec', 'cell'), may hold values from -6 to 6
- tensors: bfloat16 [16, 384, 384, 384], P('spec', 'cell'), may hold values from -0.0078125 to 0.0078125
- pair_table: int32 [4, 4], replicated, may hold values from 0 to 15, as said below
- plus_flux: float32 [4, 384, 384], P('spec'), may hold values from -0.3125 to 0.3125
- minus_flux: float32 [4, 384, 384], P('spec'), may hold values from -0.3125 to 0.3125
- face_limiter: int32 [4, 1024], P('spec', 'cell'), may hold values from 0 to 2
Outputs:
- new_field: float32 [4, 1024, 384], P('spec', 'cell')
- collision: float32 [4, 1024, 384], P('spec', 'cell')
Inputs may be any that keep to these rules, and one draw needn't show every extreme that they name: Row s of pair_table names each of the tensors s * 4 to s * 4 + 3 exactly once. `face_limiter`: 0 first order, 1 minmod slope, 2 monotonized central slope.
All inputs are finite; a program needn't handle non-finite values.
Results may differ from a plain program's by a relative error of at most 0.0004.
Values may be sent and summed in bfloat16 or wider, within the bound.
A program may use at most 64 MiB of HBM per device.

v0:
```python
import jax
import jax.numpy as jnp
from jax import lax
from jax.sharding import PartitionSpec as P


def with_halo(x, sides, width):
    for axis, dim in sides:
        size, length = (lax.axis_size(axis), x.shape[dim])
        up = [(i, (i + 1) % size) for i in range(size)]
        down = [(j, i) for i, j in up]
        last = lax.slice_in_dim(x, length - width, length, axis=dim)
        leading = lax.slice_in_dim(x, 0, width, axis=dim)
        before = lax.ppermute(last, axis, up)
        after = lax.ppermute(leading, axis, down)
        x = jnp.concatenate([before, x, after], axis=dim)
    return x


def shifted(x, axis, by):
    size = lax.axis_size(axis)
    return lax.ppermute(x, axis, [(i, (i + by) % size) for i in range(size)])


def minmod_two(first, second):
    return jnp.where(
        first * second > 0, jnp.sign(first) * jnp.minimum(jnp.abs(first), jnp.abs(second)), 0.0
    )


def minmod_three(first, second, third):
    same = (first * second > 0) & (second * third > 0)
    least = jnp.minimum(jnp.minimum(jnp.abs(first), jnp.abs(second)), jnp.abs(third))
    return jnp.where(same, jnp.sign(first) * least, 0.0)


def local(fields, tensors, pair_table, plus_flux, minus_flux, face_limiter):
    cells = fields.shape[1]
    species = lax.axis_size("spec")
    owner = lax.axis_index("spec")
    total_cells = cells * lax.axis_size("cell")
    out_modes = tensors.shape[1]
    table_row = lax.dynamic_index_in_dim(pair_table, owner, 0, keepdims=False)
    all_species = lax.all_gather(fields, "spec", axis=0, tiled=True)
    gathered = lax.all_gather(all_species, "cell", axis=1, tiled=True)
    own_rows = lax.dynamic_index_in_dim(gathered, owner, 0, keepdims=True)
    own_wide = own_rows[0].astype(jnp.float32)
    collision_part = jnp.zeros((total_cells, out_modes), jnp.float32)
    for partner in range(species):
        partner_rows = gathered[partner]
        local_pair = table_row[partner] - owner * species
        tensor = lax.dynamic_index_in_dim(tensors, local_pair, 0, keepdims=False)
        inner = jnp.einsum("cj,kij->cki", partner_rows, tensor, preferred_element_type=jnp.float32)
        collision_part = collision_part + jnp.einsum(
            "cki,ci->ck",
            inner,
            own_wide,
            precision=lax.Precision.HIGHEST,
            preferred_element_type=jnp.float32,
        )
    collision = lax.all_to_all(collision_part, "cell", split_axis=0, concat_axis=1, tiled=True)
    extended = with_halo(fields, (("cell", 1),), 2)
    wide = extended[0].astype(jnp.float32)
    prior_flag = shifted(face_limiter[:, -1:], "cell", 1)
    flags = jnp.concatenate([prior_flag, face_limiter], axis=1)[0][:, None]
    lower = wide[1:-1] - wide[:-2]
    upper = wide[2:] - wide[1:-1]
    slope_one = minmod_two(lower, upper)
    slope_two = minmod_three(2.0 * lower, 0.5 * (lower + upper), 2.0 * upper)
    zero = jnp.zeros((cells + 1, wide.shape[1]), jnp.float32)
    here = jnp.where(flags == 1, slope_one[:-1], jnp.where(flags == 2, slope_two[:-1], zero))
    there = jnp.where(flags == 1, slope_one[1:], jnp.where(flags == 2, slope_two[1:], zero))
    left_state = wide[1 : cells + 2] + 0.5 * here
    right_state = wide[2 : cells + 3] - 0.5 * there
    flux = jnp.dot(
        left_state,
        plus_flux[0],
        precision=lax.Precision.HIGHEST,
        preferred_element_type=jnp.float32,
    )
    flux = flux + jnp.dot(
        right_state,
        minus_flux[0],
        precision=lax.Precision.HIGHEST,
        preferred_element_type=jnp.float32,
    )
    center = wide[2 : cells + 2]
    new_field = center + 0.4 * (flux[:-1] - flux[1:]) + 0.5 * collision
    return (new_field[None], collision[None])


def solution(mesh):
    placed = (
        P("spec", "cell", None),
        P("spec", "cell", None, None),
        P(),
        P("spec", None, None),
        P("spec", None, None),
        P("spec", "cell"),
    )
    return jax.shard_map(
        local,
        mesh=mesh,
        in_specs=placed,
        out_specs=(P("spec", "cell", None), P("spec", "cell", None)),
        check_vma=False,
    )
```

profile of v0, /device:TPU:6, one launch (start us, length us, event | category | flops | bytes accessed | tf_op | source)
XLA Modules:
  0.0 143.1 jit_solution(16800425540163569697)
XLA Ops:
  7.2 0.0 copy-start
  7.2 0.0 all-gather.2.cloned.1.call-start
  7.2 7.0 %all_gather.6 = bf16[4,32,384]{2,1,0:T(8,128)(2,1)} all-gather(bf16[1,32,384]{2,1,0:T(8,128)(2,1)} %param.6), channel_id=1, replica_groups=mesh['cell'=32,'spec'=4] {'spec'}, dimensions={0}, use_global_device_ids=true | all-gather | bytes 122880 | tf_op jit(solution)/shard_map/all_gather | solution.py:44
  14.2 0.0 all-gather.2.cloned.1.call-update
  14.2 0.7 fusion.46
  15.0 6.6 %collective-permute-start.1 = (bf16[1,2,384]{2,1,0:T(2,128)(2,1)S(1)}, bf16[1,2,384]{2,1,0:T(2,128)(2,1)S(1)}, u32[]{:S(2)}, u32[]{:S(2)}) collective-permute-start(bf16[1,2,384]{2,1,0:T(2,128)(2,1)S(1)} %get-tuple-element.9), channel_id=1, source_target_pairs={{4,0},{8,4},{12,8},{16,12},{20,16},{24,20},{28,24},{32,28},{36,32}... | collective-permute-start | bytes 4616 | tf_op jit(solution)/shard_map/ppermute | solution.py:15
  21.6 0.0 collective-permute-start
  21.6 1.3 slice.92
  22.9 0.7 collective-permute-start.2
  23.6 0.7 constant_dynamic-slice_fusion
  24.2 0.6 fusion.47
  27.3 3.8 %collective-permute-done.2 = s32[1,1]{1,0:T(1,128)} collective-permute-done((s32[1,1]{1,0:T(1,128)}, s32[1,1]{1,0:T(1,128)}, u32[]{:S(2)}, u32[]{:S(2)}) %collective-permute-start.2) | collective-permute-done | bytes 36 | tf_op jit(solution)/shard_map/ppermute | solution.py:22
  31.1 1.4 compare_bitcast_fusion.1
  32.5 0.0 collective-permute-done.1
  32.5 0.0 collective-permute-done
  32.5 0.8 maximum_convert_fusion
  33.2 0.1 multiply_select_fusion.1
  33.3 0.0 copy-done
  33.3 0.5 fusion.13
  33.8 56.7 %all-gather.2.cloned.1.call-done = bf16[4,1024,384]{2,1,0:T(8,128)(2,1)} async-done(((bf16[4,32,384]{2,1,0:T(8,128)(2,1)}), bf16[4,1024,384]{2,1,0:T(8,128)(2,1)}) %all-gather.2.cloned.1.call-update) | async-done | bytes 3145744 | tf_op jit(solution)/shard_map/all_gather | solution.py:45
  90.5 1.2 bitcast_convert_fusion
  91.7 1.6 %copy.39 = f32[1024,384]{0,1:T(8,128)} copy(f32[1024,384]{1,0:T(8,128)S(1)} %bitcast_convert_fusion) | data formatting | bytes 3145728
  93.4 0.0 copy-start.1
  93.4 0.0 copy-start.3
  93.4 0.0 copy-start.4
  93.4 7.9 %fusion = f32[1024,12]{0,1:T(8,128)S(1)} fusion(f32[1024,384]{0,1:T(8,128)} %copy.39, bf16[4,12,384,384]{3,2,1,0:T(8,128)(2,1)} %param.7, s32[]{:T(128)S(6)} %select_n.49, bf16[4,1024,384]{2,1,0:T(8,128)(2,1)} %all-gather.2.cloned.1.call-done), kind=kOutput, calls=%fused_computation.1 | convolution fusion | flops 3633303552 | bytes 5947396 | tf_op jit(solution)/shard_map/cj,kij->cki/dot_general | solution.py:53
  101.2 0.0 copy-done.1
  101.3 0.0 copy-done.3
  101.3 0.3 copy-done.4
  101.6 5.6 %fusion.1 = f32[1024,12]{0,1:T(8,128)S(1)} fusion(f32[1024,384]{0,1:T(8,128)S(1)} %copy-done.1, bf16[4,12,384,384]{3,2,1,0:T(8,128)(2,1)S(1)} %copy-done.4, s32[]{:T(128)S(6)} %select_n.48, bf16[4,1024,384]{2,1,0:T(8,128)(2,1)S(1)} %copy-done.3), kind=kOutput, calls=%fused_computation.3 | convolution fusion | flops 3633303552 | bytes 5947396 | tf_op jit(solution)/shard_map/cj,kij->cki/dot_general | solution.py:53
  107.2 5.6 %fusion.3 = f32[1024,12]{0,1:T(8,128)S(1)} fusion(f32[1024,384]{0,1:T(8,128)S(1)} %copy-done.1, bf16[4,12,384,384]{3,2,1,0:T(8,128)(2,1)S(1)} %copy-done.4, s32[]{:T(128)S(6)} %select_n.46, bf16[4,1024,384]{2,1,0:T(8,128)(2,1)S(1)} %copy-done.3), kind=kOutput, calls=%fused_computation.7 | convolution fusion | flops 3633303552 | bytes 5947396 | tf_op jit(solution)/shard_map/cj,kij->cki/dot_general | solution.py:53
  112.8 0.0 copy-start.2
  112.8 5.6 %fusion.2 = f32[1024,12]{0,1:T(8,128)S(1)} fusion(f32[1024,384]{0,1:T(8,128)S(1)} %copy-done.1, bf16[4,12,384,384]{3,2,1,0:T(8,128)(2,1)S(1)} %copy-done.4, s32[]{:T(128)S(6)} %select_n.47, bf16[4,1024,384]{2,1,0:T(8,128)(2,1)S(1)} %copy-done.3), kind=kOutput, calls=%fused_computation.5 | convolution fusion | flops 3633303552 | bytes 5947396 | tf_op jit(solution)/shard_map/cj,kij->cki/dot_general | solution.py:53
  118.5 0.1 all_to_all.12
  118.6 0.1 copy.42
  118.7 0.8 reshape.94
  119.5 5.9 %all-to-all-start = ((f32[32,1,384]{2,1,0:T(1,128)}), f32[32,1,384]{2,1,0:T(1,128)S(1)}, u32[]{:S(2)}, u32[]{:S(2)}) async-start(f32[32,1,384]{2,1,0:T(1,128)} %reshape.94), calls=%async_computation | async-start | bytes 98304 | tf_op jit(solution)/shard_map/all_to_all | solution.py:61
  125.4 0.0 copy-done.2
  125.4 0.5 convolution_add_fusion
  125.9 7.4 %all-to-all-done = f32[32,1,384]{2,1,0:T(1,128)S(1)} async-done(((f32[32,1,384]{2,1,0:T(1,128)}), f32[32,1,384]{2,1,0:T(1,128)S(1)}, u32[]{:S(2)}, u32[]{:S(2)}) %all-to-all-start) | async-done | bytes 49184 | tf_op jit(solution)/shard_map/all_to_all | solution.py:61
  133.3 0.5 broadcast.69
  133.8 0.8 reduce.8
  134.6 0.1 reshape.95
  134.7 0.1 copy.13
  134.9 0.7 copy.14
  135.6 0.6 fusion.29
  (5 shorter events, 0.1 us)
Async XLA Ops:
  7.2 26.2 %copy-start = (f32[1,384,384]{2,1,0:T(8,128)S(1)}, f32[1,384,384]{2,1,0:T(8,128)}, u32[]{:S(2)}) copy-start(f32[1,384,384]{2,1,0:T(8,128)} %param.9) | copy-start | bytes 1769476
  7.2 83.3 %all-gather.2.cloned.1.call-start = ((), (), s32[]{:S(2)}) async-start(), calls=%async_computation.1 | async-start | bytes 3244032 | tf_op jit(solution)/shard_map/all_gather | solution.py:45
  15.0 17.5 %collective-permute-start.1 = (bf16[1,2,384]{2,1,0:T(2,128)(2,1)S(1)}, bf16[1,2,384]{2,1,0:T(2,128)(2,1)S(1)}, u32[]{:S(2)}, u32[]{:S(2)}) collective-permute-start(bf16[1,2,384]{2,1,0:T(2,128)(2,1)S(1)} %get-tuple-element.9), channel_id=1, source_target_pairs={{4,0},{8,4},{12,8},{16,12},{20,16},{24,20},{28,24},{32,28},{36,32}... | collective-permute-start | bytes 4616 | tf_op jit(solution)/shard_map/ppermute | solution.py:15
  21.6 10.9 %collective-permute-start = (bf16[1,2,384]{2,1,0:T(2,128)(2,1)S(1)}, bf16[1,2,384]{2,1,0:T(2,128)(2,1)S(1)}, u32[]{:S(2)}, u32[]{:S(2)}) collective-permute-start(bf16[1,2,384]{2,1,0:T(2,128)(2,1)S(1)} %get-tuple-element.8), channel_id=1, source_target_pairs={{0,4},{4,8},{8,12},{12,16},{16,20},{20,24},{24,28},{28,32},{32,36}... | collective-permute-start | bytes 4616 | tf_op jit(solution)/shard_map/ppermute | solution.py:14
  22.9 8.2 %collective-permute-start.2 = (s32[1,1]{1,0:T(1,128)}, s32[1,1]{1,0:T(1,128)}, u32[]{:S(2)}, u32[]{:S(2)}) collective-permute-start(s32[1,1]{1,0:T(1,128)} %slice.92), channel_id=1, source_target_pairs={{0,4},{4,8},{8,12},{12,16},{16,20},{20,24},{24,28},{28,32},{32,36}... | collective-permute-start | bytes 20 | tf_op jit(solution)/shard_map/ppermute | solution.py:22
  93.4 7.9 %copy-start.1 = (f32[1024,384]{0,1:T(8,128)S(1)}, f32[1024,384]{0,1:T(8,128)}, u32[]{:S(2)}) copy-start(f32[1024,384]{0,1:T(8,128)} %copy.39) | copy-start | bytes 4718596
  93.4 7.9 %copy-start.3 = (bf16[4,1024,384]{2,1,0:T(8,128)(2,1)S(1)}, bf16[4,1024,384]{2,1,0:T(8,128)(2,1)}, u32[]{:S(2)}) copy-start(bf16[4,1024,384]{2,1,0:T(8,128)(2,1)} %all-gather.2.cloned.1.call-done) | copy-start | bytes 9437188
  93.4 8.2 %copy-start.4 = (bf16[4,12,384,384]{3,2,1,0:T(8,128)(2,1)S(1)}, bf16[4,12,384,384]{3,2,1,0:T(8,128)(2,1)}, u32[]{:S(2)}) copy-start(bf16[4,12,384,384]{3,2,1,0:T(8,128)(2,1)} %param.7) | copy-start | bytes 42467332
  112.8 12.6 %copy-start.2 = (f32[1,384,384]{2,1,0:T(8,128)S(1)}, f32[1,384,384]{2,1,0:T(8,128)}, u32[]{:S(2)}) copy-start(f32[1,384,384]{2,1,0:T(8,128)} %param.10) | copy-start | bytes 1769476
  119.5 13.8 %all-to-all-start = ((f32[32,1,384]{2,1,0:T(1,128)}), f32[32,1,384]{2,1,0:T(1,128)S(1)}, u32[]{:S(2)}, u32[]{:S(2)}) async-start(f32[32,1,384]{2,1,0:T(1,128)} %reshape.94), calls=%async_computation | async-start | bytes 98304 | tf_op jit(solution)/shard_map/all_to_all | solution.py:61
Sparse Core Ops, SparseCore 0:
  14.4 76.0 all-gather.1
where the time goes:
time: 145 us; the launch traced here: 143 us
  waiting for transfers between devices  67.9 us (47%)
  matrix products  25.7 us (18%)
  between operations  16.7 us (12%)
  starting transfers between devices  13.3 us (9%)
  local copies, waits for them, and re-layouts  7.71 us (5%)
  blocking collectives  6.99 us (5%)
  other arithmetic  4.88 us (3%)
    all_gather x1, waiting for transfers between devices, local(): gathered = lax.all_gather(all_species, 'cell', axis=1, tiled=True)  56.7 us
    dot_general x4, matrix products, local(): jnp.einsum('cj,kij->cki', partner_rows, tensor, preferred_element_type=jn...  24.7 us
    all_to_all x1, waiting for transfers between devices, local(): lax.all_to_all(collision_part, 'cell', split_axis=0, concat_axis=1, tiled...  7.4 us
    all_gather x1, blocking collectives, local(): all_species = lax.all_gather(fields, 'spec', axis=0, tiled=True)  6.99 us
    ppermute x1, starting transfers between devices, with_halo(): after = lax.ppermute(leading, axis, down)  6.64 us
    all_to_all x1, starting transfers between devices, local(): lax.all_to_all(collision_part, 'cell', split_axis=0, concat_axis=1, tiled...  5.9 us
    ppermute x1, waiting for transfers between devices, shifted(): return lax.ppermute(x, axis, [(i, (i + by) % size) for i in range(size)])  3.77 us
    unnamed x14, local copies, waits for them, and re-layouts  3.55 us
  transfers between devices with their start and end apart: 5, of which 3 were waited for; matrix products, arithmetic and copies ran while one was open for 4% of the time, Pallas kernels for 0%

commit v1 on v0

v1 whole, which is shorter than its diff:
```python
import functools

import jax
import jax.numpy as jnp
from jax import lax
from jax.experimental import pallas as pl
from jax.experimental.pallas import tpu as pltpu
from jax.sharding import PartitionSpec as P

MESH = pl.DeviceIdType.MESH
HALF = 16
GROUP = 4


def minmod_two(first, second):
    least = jnp.minimum(jnp.abs(first), jnp.abs(second))
    return jnp.where(first * second > 0, jnp.where(first > 0, least, -least), 0.0)


def minmod_three(first, second, third):
    same = (first * second > 0) & (second * third > 0)
    least = jnp.minimum(jnp.minimum(jnp.abs(first), jnp.abs(second)), jnp.abs(third))
    return jnp.where(same, jnp.where(first > 0, least, -least), 0.0)


def mod(value, size):
    return lax.rem(value, size)


def step_kernel(
    dims,
    pair_table,
    fields,
    tensors,
    plus_hbm,
    minus_hbm,
    limiter,
    new_ref,
    coll_ref,
    held0,
    held1,
    held2,
    held3,
    a_ref,
    plus_ref,
    minus_ref,
    flag_ref,
    prior_flag,
    before,
    after,
    own_t,
    line,
    outgoing,
    incoming,
    rows,
    base,
    load_sem,
    edge_send,
    edge_recv,
    x_send,
    x_recv,
    line_send,
    line_recv,
    pair_send,
    pair_recv,
    exit_send,
    exit_recv,
):
    nx, nz, nyh, nyl, ncore = dims
    ny = nyh * nyl
    held = (held0, held1, held2, held3)
    species = nyl * ncore
    out_modes = tensors.shape[1]
    modes = tensors.shape[2]
    plane = nz * nyh
    cell = lax.axis_index("cell")
    spec = lax.axis_index("spec")
    yh = mod(cell, nyh)
    z = mod(lax.div(cell, nyh), nz)
    x = lax.div(cell, plane)
    spot = mod(cell, plane)
    yl = lax.div(spec, ncore)
    core = mod(spec, ncore)
    y = yh * nyl + yl

    def device(x_at, z_at, y_at, core_at):
        return (
            (x_at * nz + z_at) * nyh + lax.div(y_at, nyl),
            mod(y_at, nyl) * ncore + core_at,
        )

    def remote(src, dst, send, recv, to):
        return pltpu.make_async_remote_copy(
            src_ref=src,
            dst_ref=dst,
            send_sem=send,
            recv_sem=recv,
            device_id=to,
            device_id_type=MESH,
        )

    def block(q):
        return held[q].at[core, yl, z, yh]

    loads = [
        pltpu.make_async_copy(tensors.at[p], a_ref.at[p], load_sem.at[p])
        for p in range(species)
    ]
    own_load = pltpu.make_async_copy(fields.at[0], block(0), load_sem.at[4])
    flag_load = pltpu.make_async_copy(limiter, flag_ref, load_sem.at[5])
    plus_load = pltpu.make_async_copy(plus_hbm.at[0], plus_ref, load_sem.at[6])
    minus_load = pltpu.make_async_copy(minus_hbm.at[0], minus_ref, load_sem.at[7])
    own_load.start()
    flag_load.start()
    plus_load.start()
    minus_load.start()
    for load in loads:
        load.start()

    ring = nx * plane
    succ = (mod(cell + 1, ring), spec)
    pred = (mod(cell + ring - 1, ring), spec)
    greeted = [device(x, z, y, 1 - core), succ, pred]
    greeted += [device(mod(x + o, nx), z, y, core) for o in range(1, nx)]
    greeted += [device(x, mod(z + o, nz), y, core) for o in range(1, nz)]
    greeted += [device(x, z, mod(y + o, ny), core) for o in range(1, ny)]
    barrier = pltpu.get_barrier_semaphore()
    for other in greeted:
        pl.semaphore_signal(barrier, inc=1, device_id=other, device_id_type=MESH)
    own_load.wait()
    flag_load.wait()
    pl.semaphore_wait(barrier, len(greeted))

    def first(q):
        copies = []
        for o in range(1, ny):
            here = held[q].at[core, yl, z, yh, 0]
            to = device(x, z, mod(y + o, ny), core)
            copies.append((here, here, line_send.at[q, o - 1], line_recv.at[q, o - 1], to))
        for o in range(1, nz):
            here = held[q].at[core, yl, z, yh, 1]
            to = device(x, mod(z + o, nz), y, core)
            copies.append((here, here, line_send.at[q, o + 2], line_recv.at[q, o + 2], to))
        return [remote(*c) for c in copies]

    def second(q):
        copies = []
        for o in range(1, nz):
            here = held[q].at[core, :, z, :, 0]
            to = device(x, mod(z + o, nz), y, core)
            copies.append((here, here, line_send.at[q, o + 5], line_recv.at[q, o + 5], to))
        for o in range(1, ny):
            here = held[q].at[core, yl, :, yh, 1]
            to = device(x, z, mod(y + o, ny), core)
            copies.append((here, here, line_send.at[q, o + 8], line_recv.at[q, o + 8], to))
        return [remote(*c) for c in copies]

    def first_in(q):
        me = (cell, spec)
        for o in range(1, ny):
            y_from = mod(y + ny - o, ny)
            there = held[q].at[core, mod(y_from, nyl), z, lax.div(y_from, nyl), 0]
            remote(there, there, line_send.at[q, o - 1], line_recv.at[q, o - 1], me).wait_recv()
        for o in range(1, nz):
            there = held[q].at[core, yl, mod(z + nz - o, nz), yh, 1]
            remote(there, there, line_send.at[q, o + 2], line_recv.at[q, o + 2], me).wait_recv()

    def second_in(q):
        me = (cell, spec)
        for o in range(1, nz):
            there = held[q].at[core, :, mod(z + nz - o, nz), :, 0]
            remote(there, there, line_send.at[q, o + 5], line_recv.at[q, o + 5], me).wait_recv()
        for o in range(1, ny):
            y_from = mod(y + ny - o, ny)
            there = held[q].at[core, mod(y_from, nyl), :, lax.div(y_from, nyl), 1]
            remote(there, there, line_send.at[q, o + 8], line_recv.at[q, o + 8], me).wait_recv()

    def paired(q, which):
        half = held[q].at[which]
        return remote(half, half, pair_send.at[q], pair_recv.at[q], device(x, z, y, 1 - core))

    sent = []

    def go(copies):
        for copy in copies:
            copy.start()
        sent.extend(copies)

    go(
        [
            remote(held[0].at[core, yl, z, yh, 1], before, edge_send.at[0], edge_recv.at[0], succ),
            remote(held[0].at[core, yl, z, yh, 0], after, edge_send.at[1], edge_recv.at[1], pred),
            remote(flag_ref, prior_flag, edge_send.at[2], edge_recv.at[2], succ),
        ]
    )
    go(first(0))
    order = (2, 1, 3)
    go(
        [
            remote(block(0), block(q), x_send.at[q], x_recv.at[q], device(mod(x + nx - q, nx), z, y, core))
            for q in order
        ]
    )
    first_in(0)
    go(second(0))

    me = (cell, spec)
    plus_load.wait()
    minus_load.wait()
    remote(before, before, edge_send.at[0], edge_recv.at[0], me).wait_recv()
    remote(after, after, edge_send.at[1], edge_recv.at[1], me).wait_recv()
    remote(flag_ref, prior_flag, edge_send.at[2], edge_recv.at[2], me).wait_recv()
    own = held[0][core, yl, z, yh].reshape(2 * HALF, modes)
    wide = jnp.concatenate([before[...], own, after[...]], axis=0).astype(jnp.float32)
    count = 4 * HALF
    up = pltpu.roll(wide, 1, 0)
    down = pltpu.roll(wide, count - 1, 0)
    lower = wide - up
    upper = down - wide
    slope_one = minmod_two(lower, upper)
    slope_two = minmod_three(2.0 * lower, 0.5 * (lower + upper), 2.0 * upper)
    line[...] = jnp.zeros_like(line)
    line[0:1, 0 : 2 * HALF] = flag_ref[...].astype(jnp.float32)
    line[1:2, 0 : 2 * HALF] = prior_flag[...].astype(jnp.float32)
    columns = jnp.transpose(line[...])
    flags = jnp.concatenate(
        [
            columns[HALF : 2 * HALF, 1:2],
            columns[0 : 2 * HALF, 0:1],
            jnp.zeros((HALF, 1), jnp.float32),
        ],
        axis=0,
    )
    flags = jnp.broadcast_to(flags, (count, modes))
    here = jnp.where(flags == 1.0, slope_one, jnp.where(flags == 2.0, slope_two, 0.0))
    next_one = pltpu.roll(slope_one, count - 1, 0)
    next_two = pltpu.roll(slope_two, count - 1, 0)
    there = jnp.where(flags == 1.0, next_one, jnp.where(flags == 2.0, next_two, 0.0))
    left_state = (wide + 0.5 * here)[0 : 3 * HALF]
    right_state = (down - 0.5 * there)[0 : 3 * HALF]
    flux = jnp.dot(
        left_state, plus_ref[...], precision=lax.Precision.HIGHEST, preferred_element_type=jnp.float32
    ) + jnp.dot(
        right_state, minus_ref[...], precision=lax.Precision.HIGHEST, preferred_element_type=jnp.float32
    )
    change = pltpu.roll(flux, 1, 0) - flux
    base[...] = own.astype(jnp.float32) + 0.4 * change[HALF : 3 * HALF]

    def x_in(q):
        remote(block(q), block(q), x_send.at[q], x_recv.at[q], me).wait_recv()

    for q in order:
        x_in(q)
        go(first(q))
    second_in(0)
    go([paired(0, core)])
    first_in(order[0])
    go(second(order[0]))
    for load in loads:
        load.wait()
    spot_of = [mod(pair_table[spec, t], species) for t in range(species)]

    def exits(q):
        copies = []
        for j in range(plane):
            if q == 0 and j == 0:
                continue
            d = mod(spot + j, plane)
            to = (mod(x + q, nx) * plane + d, spec)
            copies.append(
                remote(outgoing.at[q, d], incoming.at[cell], exit_send.at[q, j], exit_recv.at[q, j], to)
            )
        return copies

    chunks = (0,) + order
    parts = out_modes // GROUP
    for at, q in enumerate(chunks):
        paired(q, 1 - core).wait_recv()
        own_t[...] = jnp.transpose(
            held[q][core, yl].reshape(plane * 2 * HALF, modes).astype(jnp.float32)
        )
        for g in range(parts):
            pieces = [held[q][t % ncore, t // ncore].reshape(plane * 2 * HALF, modes) for t in range(species)]
            right = jnp.concatenate(pieces, axis=1)
            left = jnp.concatenate(
                [
                    jnp.concatenate([a_ref[spot_of[t], GROUP * g + u] for t in range(species)], axis=1)
                    for u in range(GROUP)
                ],
                axis=0,
            )
            inner = lax.dot_general(
                left, right, (((1,), (1,)), ((), ())), preferred_element_type=jnp.float32
            )
            for u in range(GROUP):
                k = GROUP * g + u
                rows[k : k + 1, :] = jnp.sum(
                    inner[modes * u : modes * (u + 1)] * own_t[...], axis=0, keepdims=True
                )
            if g == 0 and at + 1 < len(chunks):
                second_in(chunks[at + 1])
                go([paired(chunks[at + 1], core)])
            if g == 0 and at + 2 < len(chunks):
                first_in(chunks[at + 2])
                go(second(chunks[at + 2]))
        whole = rows[...]
        width = plane * 2 * HALF
        for d in range(plane):
            turned = whole if d == 0 else pltpu.roll(whole, width - 2 * HALF * d, 1)
            outgoing[q, d] = turned[:, 0:128]
        go(exits(q))
    incoming[cell] = outgoing[0, spot]
    for q in range(nx):
        for j in range(plane):
            if q == 0 and j == 0:
                continue
            source = mod(x + nx - q, nx) * plane + mod(spot + plane - j, plane)
            slot = incoming.at[source]
            remote(slot, slot, exit_send.at[q, j], exit_recv.at[q, j], me).wait_recv()
    table = jnp.concatenate([incoming[i] for i in range(ring)], axis=0)
    collision = jnp.transpose(table)[0 : 2 * HALF]
    coll_ref[0] = collision
    new_ref[0] = base[...] + 0.5 * collision
    for copy in sent:
        copy.wait_send()


def local(dims, fields, tensors, pair_table, plus_flux, minus_flux, face_limiter):
    nx, nz, nyh, nyl, ncore = dims
    _, cells, modes = fields.shape
    out_modes = tensors.shape[1]
    plane = nz * nyh
    ring = nx * plane
    width = plane * cells
    dma = pltpu.SemaphoreType.DMA
    held = pltpu.VMEM((ncore, nyl, nz, nyh, 2, HALF, modes), jnp.bfloat16)
    any_space = pl.BlockSpec(memory_space=pl.ANY)
    fields = fields.reshape(1, 2, HALF, modes)
    return pl.pallas_call(
        functools.partial(step_kernel, dims),
        out_shape=(
            jax.ShapeDtypeStruct((1, cells, modes), jnp.float32),
            jax.ShapeDtypeStruct((1, cells, modes), jnp.float32),
        ),
        in_specs=[pl.BlockSpec(memory_space=pltpu.SMEM)] + [any_space] * 5,
        out_specs=(pl.BlockSpec(memory_space=pltpu.VMEM),) * 2,
        scratch_shapes=[
            held,
            held,
            held,
            held,
            pltpu.VMEM(tensors.shape, jnp.bfloat16),
            pltpu.VMEM((modes, modes), jnp.float32),
            pltpu.VMEM((modes, modes), jnp.float32),
            pltpu.VMEM((1, cells), jnp.int32),
            pltpu.VMEM((1, cells), jnp.int32),
            pltpu.VMEM((HALF, modes), jnp.bfloat16),
            pltpu.VMEM((HALF, modes), jnp.bfloat16),
            pltpu.VMEM((modes, width), jnp.float32),
            pltpu.VMEM((8, 128), jnp.float32),
            pltpu.VMEM((nx, plane, out_modes, 128), jnp.float32),
            pltpu.VMEM((ring, out_modes, 128), jnp.float32),
            pltpu.VMEM((out_modes, width), jnp.float32),
            pltpu.VMEM((cells, modes), jnp.float32),
            dma((8,)),
            dma((3,)),
            dma((3,)),
            dma((nx,)),
            dma((nx,)),
            dma((nx, 12)),
            dma((nx, 12)),
            dma((nx,)),
            dma((nx,)),
            dma((nx, plane)),
            dma((nx, plane)),
        ],
        compiler_params=pltpu.CompilerParams(
            collective_id=0, has_side_effects=True, vmem_limit_bytes=60 * 2**20
        ),
        name="step",
    )(pair_table, fields, tensors, plus_flux, minus_flux, face_limiter)


def solution(mesh):
    placed = (
        P("spec", "cell", None),
        P("spec", "cell", None, None),
        P(),
        P("spec", None, None),
        P("spec", None, None),
        P("spec", "cell"),
    )
    dims = (4, 4, 2, 2, 2)
    return jax.shard_map(
        functools.partial(local, dims),
        mesh=mesh,
        in_specs=placed,
        out_specs=(P("spec", "cell", None), P("spec", "cell", None)),
        check_vma=False,
    )
```

time: 145 us -> 54.3 us (0.37)
  the two profiles are of different devices: /device:TPU:6 before, /device:TPU:4 now
where the time goes in v1:
time: 54.3 us; the launch traced here: 54.1 us
  Pallas kernels  50.6 us (93%)
  local copies, waits for them, and re-layouts  2.84 us (5%)
  between operations  0.64 us (1%)
    pallas_call x1, Pallas kernels, local(): pl.pallas_call(functools.partial(step_kernel, dims), out_shape=(jax.Shape...  50.6 us
    unnamed x2, local copies, waits for them, and re-layouts  2.84 us

profile of v1, /device:TPU:4, one launch (start us, length us, event | category | flops | bytes accessed | tf_op | source)
XLA Modules:
  0.0 54.1 jit_solution(8498424432561087178)
XLA Ops:
  0.6 50.6 %step.1 = (f32[1,32,384]{2,1,0:T(8,128)}, f32[1,32,384]{2,1,0:T(8,128)}) custom-call(s32[4,4]{1,0:T(4,128)} %pair_table.1, bf16[1,2,16,384]{3,2,1,0:T(8,128)(2,1)} %bitcast.1, bf16[4,12,384,384]{3,2,1,0:T(8,128)(2,1)} %tensors.1, f32[1,384,384]{2,1,0:T(8,128)} %plus_hbm.1, f32[1,384,384]{2,1,0:T(8,128)} %minus_hbm.1, s32[1,32]{1,0:T(1,128)} %limiter.1), custom_call_target="tpu_custom_call" | custom-call | tf_op jit(solution)/shard_map/step/pallas_call | solution.py:339
  51.2 1.4 %copy.10 = f32[1,32,384]{2,1,0:T(8,128)} copy(f32[1,32,384]{2,1,0:T(8,128)} %get-tuple-element.4) | data formatting | bytes 98304
  52.7 1.4 %copy.11 = f32[1,32,384]{2,1,0:T(8,128)} copy(f32[1,32,384]{2,1,0:T(8,128)} %get-tuple-element.5) | data formatting | bytes 98304

commit v2 on v1

--- a/solution.py
+++ b/solution.py
@@ -10,6 +10,7 @@
 MESH = pl.DeviceIdType.MESH
 HALF = 16
 GROUP = 4
+STRETCHES = ((0,), (2, 1), (3,))
 
 
 def minmod_two(first, second):
@@ -29,7 +30,7 @@
 
 def step_kernel(
     dims,
-    pair_table,
+    table_hbm,
     fields,
     tensors,
     plus_hbm,
@@ -54,6 +55,7 @@
     incoming,
     rows,
     base,
+    pair_table,
     load_sem,
     edge_send,
     edge_recv,
@@ -110,10 +112,12 @@
     flag_load = pltpu.make_async_copy(limiter, flag_ref, load_sem.at[5])
     plus_load = pltpu.make_async_copy(plus_hbm.at[0], plus_ref, load_sem.at[6])
     minus_load = pltpu.make_async_copy(minus_hbm.at[0], minus_ref, load_sem.at[7])
+    table_load = pltpu.make_async_copy(table_hbm, pair_table, load_sem.at[8])
     own_load.start()
     flag_load.start()
     plus_load.start()
     minus_load.start()
+    table_load.start()
     for load in loads:
         load.start()
 
@@ -186,6 +190,23 @@
             copy.start()
         sent.extend(copies)
 
+    me = (cell, spec)
+
+    def x_out(q):
+        to = device(mod(x + nx - q, nx), z, y, core)
+        return remote(block(0), block(q), x_send.at[q], x_recv.at[q], to)
+
+    def x_in(q):
+        remote(block(q), block(q), x_send.at[q], x_recv.at[q], me).wait_recv()
+
+    far = sum(STRETCHES[1:], ())
+    go(first(0))
+    go([x_out(q) for q in far])
+    first_in(0)
+    go(second(0))
+    for q in far:
+        x_in(q)
+        go(first(q))
     go(
         [
             remote(held[0].at[core, yl, z, yh, 1], before, edge_send.at[0], edge_recv.at[0], succ),
@@ -193,18 +214,63 @@
             remote(flag_ref, prior_flag, edge_send.at[2], edge_recv.at[2], succ),
         ]
     )
-    go(first(0))
-    order = (2, 1, 3)
-    go(
-        [
-            remote(block(0), block(q), x_send.at[q], x_recv.at[q], device(mod(x + nx - q, nx), z, y, core))
-            for q in order
-        ]
-    )
-    first_in(0)
-    go(second(0))
-
-    me = (cell, spec)
+    second_in(0)
+    go([paired(0, core)])
+    for q in far:
+        first_in(q)
+        go(second(q))
+    table_load.wait()
+    for load in loads:
+        load.wait()
+    spot_of = [mod(pair_table[spec, t], species) for t in range(species)]
+
+    def exits(q):
+        copies = []
+        for j in range(plane):
+            if q == 0 and j == 0:
+                continue
+            d = mod(spot + j, plane)
+            to = (mod(x + q, nx) * plane + d, spec)
+            copies.append(
+                remote(outgoing.at[q, d], incoming.at[cell], exit_send.at[q, j], exit_recv.at[q, j], to)
+            )
+        return copies
+
+    parts = out_modes // GROUP
+    width = plane * 2 * HALF
+    for at, stretch in enumerate(STRETCHES):
+        if at == 1:
+            for q in far:
+                second_in(q)
+                go([paired(q, core)])
+        for q in stretch:
+            paired(q, 1 - core).wait_recv()
+        for q in stretch:
+            own_t[q] = jnp.transpose(held[q][core, yl].reshape(width, modes).astype(jnp.float32))
+            pieces = [held[q][t % ncore, t // ncore].reshape(width, modes) for t in range(species)]
+            right = jnp.concatenate(pieces, axis=1)
+            for g in range(parts):
+                left = jnp.concatenate(
+                    [
+                        jnp.concatenate([a_ref[spot_of[t], GROUP * g + u] for t in range(species)], axis=1)
+                        for u in range(GROUP)
+                    ],
+                    axis=0,
+                )
+                inner = lax.dot_general(
+                    left, right, (((1,), (1,)), ((), ())), preferred_element_type=jnp.float32
+                )
+                for u in range(GROUP):
+                    k = GROUP * g + u
+                    rows[q, k : k + 1, :] = jnp.sum(
+                        inner[modes * u : modes * (u + 1)] * own_t[q], axis=0, keepdims=True
+                    )
+            whole = rows[q]
+            for d in range(plane):
+                turned = whole if d == 0 else pltpu.roll(whole, width - 2 * HALF * d, 1)
+                outgoing[q, d] = turned[:, 0:128]
+        for q in stretch:
+            go(exits(q))
     plus_load.wait()
     minus_load.wait()
     remote(before, before, edge_send.at[0], edge_recv.at[0], me).wait_recv()
@@ -246,69 +312,7 @@
     change = pltpu.roll(flux, 1, 0) - flux
     base[...] = own.astype(jnp.float32) + 0.4 * change[HALF : 3 * HALF]
 
-    def x_in(q):
-        remote(block(q), block(q), x_send.at[q], x_recv.at[q], me).wait_recv()
-
-    for q in order:
-        x_in(q)
-        go(first(q))
-    second_in(0)
-    go([paired(0, core)])
-    first_in(order[0])
-    go(second(order[0]))
-    for load in loads:
-        load.wait()
-    spot_of = [mod(pair_table[spec, t], species) for t in range(species)]
-
-    def exits(q):
-        copies = []
-        for j in range(plane):
-            if q == 0 and j == 0:
-                continue
-            d = mod(spot + j, plane)
-            to = (mod(x + q, nx) * plane + d, spec)
-            copies.append(
-                remote(outgoing.at[q, d], incoming.at[cell], exit_send.at[q, j], exit_recv.at[q, j], to)
-            )
-        return copies
-
-    chunks = (0,) + order
-    parts = out_modes // GROUP
-    for at, q in enumerate(chunks):
-        paired(q, 1 - core).wait_recv()
-        own_t[...] = jnp.transpose(
-            held[q][core, yl].reshape(plane * 2 * HALF, modes).astype(jnp.float32)
-        )
-        for g in range(parts):
-            pieces = [held[q][t % ncore, t // ncore].reshape(plane * 2 * HALF, modes) for t in range(species)]
-            right = jnp.concatenate(pieces, axis=1)
-            left = jnp.concatenate(
-                [
-                    jnp.concatenate([a_ref[spot_of[t], GROUP * g + u] for t in range(species)], axis=1)
-                    for u in range(GROUP)
-                ],
-                axis=0,
-            )
-            inner = lax.dot_general(
-                left, right, (((1,), (1,)), ((), ())), preferred_element_type=jnp.float32
-            )
-            for u in range(GROUP):
-                k = GROUP * g + u
-                rows[k : k + 1, :] = jnp.sum(
-                    inner[modes * u : modes * (u + 1)] * own_t[...], axis=0, keepdims=True
-                )
-            if g == 0 and at + 1 < len(chunks):
-                second_in(chunks[at + 1])
-                go([paired(chunks[at + 1], core)])
-            if g == 0 and at + 2 < len(chunks):
-                first_in(chunks[at + 2])
-                go(second(chunks[at + 2]))
-        whole = rows[...]
-        width = plane * 2 * HALF
-        for d in range(plane):
-            turned = whole if d == 0 else pltpu.roll(whole, width - 2 * HALF * d, 1)
-            outgoing[q, d] = turned[:, 0:128]
-        go(exits(q))
+
     incoming[cell] = outgoing[0, spot]
     for q in range(nx):
         for j in range(plane):
@@ -334,15 +338,16 @@
     width = plane * cells
     dma = pltpu.SemaphoreType.DMA
     held = pltpu.VMEM((ncore, nyl, nz, nyh, 2, HALF, modes), jnp.bfloat16)
-    any_space = pl.BlockSpec(memory_space=pl.ANY)
+    in_hbm = pl.BlockSpec(memory_space=pltpu.HBM)
     fields = fields.reshape(1, 2, HALF, modes)
+    operands = (pair_table, fields, tensors, plus_flux, minus_flux, face_limiter)
     return pl.pallas_call(
         functools.partial(step_kernel, dims),
         out_shape=(
             jax.ShapeDtypeStruct((1, cells, modes), jnp.float32),
             jax.ShapeDtypeStruct((1, cells, modes), jnp.float32),
         ),
-        in_specs=[pl.BlockSpec(memory_space=pltpu.SMEM)] + [any_space] * 5,
+        in_specs=[in_hbm] * 6,
         out_specs=(pl.BlockSpec(memory_space=pltpu.VMEM),) * 2,
         scratch_shapes=[
             held,
@@ -356,13 +361,14 @@
             pltpu.VMEM((1, cells), jnp.int32),
             pltpu.VMEM((HALF, modes), jnp.bfloat16),
             pltpu.VMEM((HALF, modes), jnp.bfloat16),
-            pltpu.VMEM((modes, width), jnp.float32),
+            pltpu.VMEM((nx, modes, width), jnp.float32),
             pltpu.VMEM((8, 128), jnp.float32),
             pltpu.VMEM((nx, plane, out_modes, 128), jnp.float32),
             pltpu.VMEM((ring, out_modes, 128), jnp.float32),
-            pltpu.VMEM((out_modes, width), jnp.float32),
+            pltpu.VMEM((nx, out_modes, width), jnp.float32),
             pltpu.VMEM((cells, modes), jnp.float32),
-            dma((8,)),
+            pltpu.SMEM(pair_table.shape, jnp.int32),
+            dma((9,)),
             dma((3,)),
             dma((3,)),
             dma((nx,)),
@@ -375,10 +381,10 @@
             dma((nx, plane)),
         ],
         compiler_params=pltpu.CompilerParams(
-            collective_id=0, has_side_effects=True, vmem_limit_bytes=60 * 2**20
+            collective_id=0, has_side_effects=True, vmem_limit_bytes=40 * 2**20
         ),
         name="step",
-    )(pair_table, fields, tensors, plus_flux, minus_flux, face_limiter)
+    )(*[pltpu.with_memory_space_constraint(v, pltpu.HBM) for v in operands])
 
 
 def solution(mesh):

time: 54.3 us -> 47.6 us (0.88)
  the two profiles are of different devices: /device:TPU:4 before, /device:TPU:6 now
where the time goes in v2:
time: 47.6 us; the launch traced here: 47.5 us
  Pallas kernels  45.6 us (96%)
  local copies, waits for them, and re-layouts  1.24 us (3%)
  between operations  0.64 us (1%)
    pallas_call x1, Pallas kernels, local(): pl.pallas_call(functools.partial(step_kernel, dims), out_shape=(jax.Shape...  45.6 us
    unnamed x2, local copies, waits for them, and re-layouts  1.24 us

profile of v2, /device:TPU:6, one launch (start us, length us, event | category | flops | bytes accessed | tf_op | source)
XLA Modules:
  0.0 47.5 jit_solution(15524776202586033485)
XLA Ops:
  0.6 45.6 %step.1 = (f32[1,32,384]{2,1,0:T(8,128)S(1)}, f32[1,32,384]{2,1,0:T(8,128)S(1)}) custom-call(s32[4,4]{1,0:T(4,128)} %table_hbm.1, bf16[1,2,16,384]{3,2,1,0:T(8,128)(2,1)} %bitcast.1, bf16[4,12,384,384]{3,2,1,0:T(8,128)(2,1)} %tensors.1, f32[1,384,384]{2,1,0:T(8,128)} %plus_hbm.1, f32[1,384,384]{2,1,0:T(8,128)} %minus_hbm.1, s32[1,32]{1,0:T(1,128)} %limiter.1), custom_call_target="tpu_custom_call" | custom-call | tf_op jit(solution)/shard_map/step/pallas_call | solution.py:344
  46.3 0.6 %copy.10 = f32[1,32,384]{2,1,0:T(8,128)} copy(f32[1,32,384]{2,1,0:T(8,128)S(1)} %get-tuple-element.4) | data formatting | bytes 98304
  46.9 0.6 %copy.11 = f32[1,32,384]{2,1,0:T(8,128)} copy(f32[1,32,384]{2,1,0:T(8,128)S(1)} %get-tuple-element.5) | data formatting | bytes 98304

commit v3 on v2

--- a/solution.py
+++ b/solution.py
@@ -9,8 +9,8 @@
 
 MESH = pl.DeviceIdType.MESH
 HALF = 16
-GROUP = 4
-STRETCHES = ((0,), (2, 1), (3,))
+GROUP = 3
+FARTHEST = (2, 1, 3)
 
 
 def minmod_two(first, second):
@@ -137,11 +137,11 @@
 
     def first(q):
         copies = []
-        for o in range(1, ny):
+        for o in FARTHEST:
             here = held[q].at[core, yl, z, yh, 0]
             to = device(x, z, mod(y + o, ny), core)
             copies.append((here, here, line_send.at[q, o - 1], line_recv.at[q, o - 1], to))
-        for o in range(1, nz):
+        for o in FARTHEST:
             here = held[q].at[core, yl, z, yh, 1]
             to = device(x, mod(z + o, nz), y, core)
             copies.append((here, here, line_send.at[q, o + 2], line_recv.at[q, o + 2], to))
@@ -149,11 +149,11 @@
 
     def second(q):
         copies = []
-        for o in range(1, nz):
+        for o in FARTHEST:
             here = held[q].at[core, :, z, :, 0]
             to = device(x, mod(z + o, nz), y, core)
             copies.append((here, here, line_send.at[q, o + 5], line_recv.at[q, o + 5], to))
-        for o in range(1, ny):
+        for o in FARTHEST:
             here = held[q].at[core, yl, :, yh, 1]
             to = device(x, z, mod(y + o, ny), core)
             copies.append((here, here, line_send.at[q, o + 8], line_recv.at[q, o + 8], to))
@@ -199,7 +199,8 @@
     def x_in(q):
         remote(block(q), block(q), x_send.at[q], x_recv.at[q], me).wait_recv()
 
-    far = sum(STRETCHES[1:], ())
+    chunks = (0, 2, 1, 3)
+    far = chunks[1:]
     go(first(0))
     go([x_out(q) for q in far])
     first_in(0)
@@ -238,39 +239,38 @@
 
     parts = out_modes // GROUP
     width = plane * 2 * HALF
-    for at, stretch in enumerate(STRETCHES):
-        if at == 1:
-            for q in far:
-                second_in(q)
-                go([paired(q, core)])
-        for q in stretch:
-            paired(q, 1 - core).wait_recv()
-        for q in stretch:
-            own_t[q] = jnp.transpose(held[q][core, yl].reshape(width, modes).astype(jnp.float32))
-            pieces = [held[q][t % ncore, t // ncore].reshape(width, modes) for t in range(species)]
-            right = jnp.concatenate(pieces, axis=1)
-            for g in range(parts):
-                left = jnp.concatenate(
-                    [
-                        jnp.concatenate([a_ref[spot_of[t], GROUP * g + u] for t in range(species)], axis=1)
-                        for u in range(GROUP)
-                    ],
-                    axis=0,
+    paired(0, 1 - core).wait_recv()
+    for at, q in enumerate(chunks):
+        own_t[q] = jnp.transpose(held[q][core, yl].reshape(width, modes).astype(jnp.float32))
+        pieces = [held[q][t % ncore, t // ncore].reshape(width, modes) for t in range(species)]
+        right = jnp.concatenate(pieces, axis=1)
+        for g in range(parts):
+            left = jnp.concatenate(
+                [
+                    jnp.concatenate([a_ref[spot_of[t], GROUP * g + u] for t in range(species)], axis=1)
+                    for u in range(GROUP)
+                ],
+                axis=0,
+            )
+            inner = lax.dot_general(
+                left, right, (((1,), (1,)), ((), ())), preferred_element_type=jnp.float32
+            )
+            for u in range(GROUP):
+                k = GROUP * g + u
+                rows[q, k : k + 1, :] = jnp.sum(
+                    inner[modes * u : modes * (u + 1)] * own_t[q], axis=0, keepdims=True
                 )
-                inner = lax.dot_general(
-                    left, right, (((1,), (1,)), ((), ())), preferred_element_type=jnp.float32
-                )
-                for u in range(GROUP):
-                    k = GROUP * g + u
-                    rows[q, k : k + 1, :] = jnp.sum(
-                        inner[modes * u : modes * (u + 1)] * own_t[q], axis=0, keepdims=True
-                    )
-            whole = rows[q]
-            for d in range(plane):
-                turned = whole if d == 0 else pltpu.roll(whole, width - 2 * HALF * d, 1)
-                outgoing[q, d] = turned[:, 0:128]
-        for q in stretch:
-            go(exits(q))
+            if g == 1 and at < 2:
+                for later in chunks[1:2] if at == 0 else chunks[2:]:
+                    second_in(later)
+                    go([paired(later, core)])
+        whole = rows[q]
+        for d in range(plane):
+            turned = whole if d == 0 else pltpu.roll(whole, width - 2 * HALF * d, 1)
+            outgoing[q, d] = turned[:, 0:128]
+        go(exits(q))
+        if at + 1 < len(chunks):
+            paired(chunks[at + 1], 1 - core).wait_recv()
     plus_load.wait()
     minus_load.wait()
     remote(before, before, edge_send.at[0], edge_recv.at[0], me).wait_recv()
@@ -324,9 +324,14 @@
     table = jnp.concatenate([incoming[i] for i in range(ring)], axis=0)
     collision = jnp.transpose(table)[0 : 2 * HALF]
     coll_ref[0] = collision
-    new_ref[0] = base[...] + 0.5 * collision
+    new_ref[0] = base[...]
     for copy in sent:
         copy.wait_send()
+
+
+def finish(kept, collision, new_ref, coll_ref):
+    coll_ref[...] = collision[...]
+    new_ref[...] = kept[...] + 0.5 * collision[...]
 
 
 def local(dims, fields, tensors, pair_table, plus_flux, minus_flux, face_limiter):
@@ -341,7 +346,7 @@
     in_hbm = pl.BlockSpec(memory_space=pltpu.HBM)
     fields = fields.reshape(1, 2, HALF, modes)
     operands = (pair_table, fields, tensors, plus_flux, minus_flux, face_limiter)
-    return pl.pallas_call(
+    kept, collision = pl.pallas_call(
         functools.partial(step_kernel, dims),
         out_shape=(
             jax.ShapeDtypeStruct((1, cells, modes), jnp.float32),
@@ -385,6 +390,17 @@
         ),
         name="step",
     )(*[pltpu.with_memory_space_constraint(v, pltpu.HBM) for v in operands])
+    return pl.pallas_call(
+        finish,
+        out_shape=(
+            jax.ShapeDtypeStruct((1, cells, modes), jnp.float32),
+            jax.ShapeDtypeStruct((1, cells, modes), jnp.float32),
+        ),
+        in_specs=[pl.BlockSpec(memory_space=pltpu.VMEM)] * 2,
+        out_specs=(pl.BlockSpec(memory_space=pltpu.VMEM),) * 2,
+        compiler_params=pltpu.CompilerParams(vmem_limit_bytes=2**20),
+        name="finish",
+    )(kept, collision)
 
 
 def solution(mesh):

time: 47.6 us -> 44 us (0.924)
  Pallas kernels: 45.6 us -> 43.2 us
  local copies, waits for them, and re-layouts: 1.24 us -> 0 us
    pallas_call x1, Pallas kernels: 45.6 us -> 42.6 us  [local(): pl.pallas_call(functools.partial(step_kernel, dims), out_shape=(jax.Shape...]
    unnamed x2 -> x0, local copies, waits for them, and re-layouts: 1.24 us -> none
    pallas_call x0 -> x1, Pallas kernels: none -> 0.65 us  [local(): pl.pallas_call(finish, out_shape=(jax.ShapeDtypeStruct((1, cells, modes),...]
where the time goes in v3:
time: 44 us; the launch traced here: 43.9 us
  Pallas kernels  43.2 us (98%)
  between operations  0.64 us (1%)
    pallas_call x1, Pallas kernels, local(): pl.pallas_call(functools.partial(step_kernel, dims), out_shape=(jax.Shape...  42.6 us

profile of v3, /device:TPU:6, one launch (start us, length us, event | category | flops | bytes accessed | tf_op | source)
XLA Modules:
  0.0 43.9 jit_solution(11080865529396471853)
XLA Ops:
  0.6 42.6 %step.1 = (f32[1,32,384]{2,1,0:T(8,128)S(1)}, f32[1,32,384]{2,1,0:T(8,128)S(1)}) custom-call(s32[4,4]{1,0:T(4,128)} %table_hbm.1, bf16[1,2,16,384]{3,2,1,0:T(8,128)(2,1)} %bitcast.1, bf16[4,12,384,384]{3,2,1,0:T(8,128)(2,1)} %tensors.1, f32[1,384,384]{2,1,0:T(8,128)} %plus_hbm.1, f32[1,384,384]{2,1,0:T(8,128)} %minus_hbm.1, s32[1,32]{1,0:T(1,128)} %limiter.1), custom_call_target="tpu_custom_call" | custom-call | tf_op jit(solution)/shard_map/step/pallas_call | solution.py:349
  43.2 0.6 %finish.1 = (f32[1,32,384]{2,1,0:T(8,128)}, f32[1,32,384]{2,1,0:T(8,128)}) custom-call(f32[1,32,384]{2,1,0:T(8,128)S(1)} %get-tuple-element.4.kept, f32[1,32,384]{2,1,0:T(8,128)S(1)} %get-tuple-element.5.collision), custom_call_target="tpu_custom_call" | custom-call | tf_op jit(solution)/shard_map/finish/pallas_call | solution.py:393

commit v4 on v3

--- a/solution.py
+++ b/solution.py
@@ -9,7 +9,7 @@
 
 MESH = pl.DeviceIdType.MESH
 HALF = 16
-GROUP = 3
+WIDE = 3
 FARTHEST = (2, 1, 3)
 
 
@@ -223,7 +223,6 @@
     table_load.wait()
     for load in loads:
         load.wait()
-    spot_of = [mod(pair_table[spec, t], species) for t in range(species)]
 
     def exits(q):
         copies = []
@@ -237,40 +236,49 @@
             )
         return copies
 
-    parts = out_modes // GROUP
     width = plane * 2 * HALF
-    paired(0, 1 - core).wait_recv()
-    for at, q in enumerate(chunks):
-        own_t[q] = jnp.transpose(held[q][core, yl].reshape(width, modes).astype(jnp.float32))
-        pieces = [held[q][t % ncore, t // ncore].reshape(width, modes) for t in range(species)]
+    def stretch(q, cores, size, fresh):
+        pieces = [held[q][c, l].reshape(width, modes) for c in cores for l in range(nyl)]
         right = jnp.concatenate(pieces, axis=1)
-        for g in range(parts):
+        spots = [mod(pair_table[spec, l * ncore + c], species) for c in cores for l in range(nyl)]
+        for g in range(out_modes // size):
             left = jnp.concatenate(
                 [
-                    jnp.concatenate([a_ref[spot_of[t], GROUP * g + u] for t in range(species)], axis=1)
-                    for u in range(GROUP)
+                    jnp.concatenate([a_ref[spot, size * g + u] for spot in spots], axis=1)
+                    for u in range(size)
                 ],
                 axis=0,
             )
             inner = lax.dot_general(
                 left, right, (((1,), (1,)), ((), ())), preferred_element_type=jnp.float32
             )
-            for u in range(GROUP):
-                k = GROUP * g + u
-                rows[q, k : k + 1, :] = jnp.sum(
-                    inner[modes * u : modes * (u + 1)] * own_t[q], axis=0, keepdims=True
-                )
-            if g == 1 and at < 2:
-                for later in chunks[1:2] if at == 0 else chunks[2:]:
+            for u in range(size):
+                k = size * g + u
+                row = jnp.sum(inner[modes * u : modes * (u + 1)] * own_t[q], axis=0, keepdims=True)
+                rows[q, k : k + 1, :] = row if fresh else rows[q, k : k + 1, :] + row
+
+    for at, q in enumerate(chunks):
+        if at == 1:
+            second_in(q)
+            go([paired(q, core)])
+        if at > 1:
+            paired(q, 1 - core).wait_recv()
+        own_t[q] = jnp.transpose(held[q][core, yl].reshape(width, modes).astype(jnp.float32))
+        if at < 2:
+            stretch(q, (core,), WIDE, True)
+            if at == 1:
+                for later in chunks[2:]:
                     second_in(later)
                     go([paired(later, core)])
+            paired(q, 1 - core).wait_recv()
+            stretch(q, (1 - core,), WIDE, False)
+        else:
+            stretch(q, (0, 1), WIDE, True)
         whole = rows[q]
         for d in range(plane):
             turned = whole if d == 0 else pltpu.roll(whole, width - 2 * HALF * d, 1)
             outgoing[q, d] = turned[:, 0:128]
         go(exits(q))
-        if at + 1 < len(chunks):
-            paired(chunks[at + 1], 1 - core).wait_recv()
     plus_load.wait()
     minus_load.wait()
     remote(before, before, edge_send.at[0], edge_recv.at[0], me).wait_recv()

time: 44 us -> 42.5 us (0.966)
  Pallas kernels: 43.2 us -> 41.7 us
    pallas_call x1, Pallas kernels: 42.6 us -> 41 us  [local(): pl.pallas_call(functools.partial(step_kernel, dims), out_shape=(jax.Shape...]
where the time goes in v4:
time: 42.5 us; the launch traced here: 42.3 us
  Pallas kernels  41.7 us (98%)
  between operations  0.64 us (2%)
    pallas_call x1, Pallas kernels, local(): pl.pallas_call(functools.partial(step_kernel, dims), out_shape=(jax.Shape...  41 us

profile of v4, /device:TPU:6, one launch (start us, length us, event | category | flops | bytes accessed | tf_op | source)
XLA Modules:
  0.0 42.3 jit_solution(6376529581258738129)
XLA Ops:
  0.6 41.0 %step.1 = (f32[1,32,384]{2,1,0:T(8,128)S(1)}, f32[1,32,384]{2,1,0:T(8,128)S(1)}) custom-call(s32[4,4]{1,0:T(4,128)} %table_hbm.1, bf16[1,2,16,384]{3,2,1,0:T(8,128)(2,1)} %bitcast.1, bf16[4,12,384,384]{3,2,1,0:T(8,128)(2,1)} %tensors.1, f32[1,384,384]{2,1,0:T(8,128)} %plus_hbm.1, f32[1,384,384]{2,1,0:T(8,128)} %minus_hbm.1, s32[1,32]{1,0:T(1,128)} %limiter.1), custom_call_target="tpu_custom_call" | custom-call | tf_op jit(solution)/shard_map/step/pallas_call | solution.py:357
  41.7 0.6 %finish.1 = (f32[1,32,384]{2,1,0:T(8,128)}, f32[1,32,384]{2,1,0:T(8,128)}) custom-call(f32[1,32,384]{2,1,0:T(8,128)S(1)} %get-tuple-element.4.kept, f32[1,32,384]{2,1,0:T(8,128)S(1)} %get-tuple-element.5.collision), custom_call_target="tpu_custom_call" | custom-call | tf_op jit(solution)/shard_map/finish/pallas_call | solution.py:401
